TPU v7x, 256 devices: a whole 4x4x8 slice. The times are simulated.
256 devices in a mesh: seq: 32 (over x_lo, z, core), chan: 8 (over x_hi, y).
Axes of the slice: x: 4 (x_hi: 2, x_lo: 2; x = x_hi * 2 + x_lo), y: 4, z: 8, core: 2. Of those that a mesh axis runs over, the one named last changes fastest.
Arguments:
- inputs: bfloat16 [262144, 1024], P('seq', 'chan'), may hold values from -6 to 6
- out_grad: bfloat16 [262144, 1024], P('seq', 'chan'), may hold values from -6 to 6
- kernel: bfloat16 [512, 512, 1024], P('seq', None, 'chan'), may hold values from -4 to 4
- gate_weight: bfloat16 [1024, 1024], P(None, 'chan'), may hold values from -0.1875 to 0.1875
- right_factor: bfloat16 [512, 512], replicated, may hold values from -0.25 to 0.25
- left_factor: bfloat16 [512, 512], replicated, may hold values from -0.25 to 0.25
Outputs:
- input_grad: bfloat16 [262144, 1024], P('seq', 'chan')
- kernel_grad: bfloat16 [512, 512, 1024], P('seq', None, 'chan')
- right_grad: float32 [262144], P(('seq', 'chan'))
- left_grad: float32 [262144], P(('seq', 'chan'))
- gate_weight_grad: float32 [1024, 1024], P(('seq', 'chan'))
All inputs are finite; a program needn't handle non-finite values.
Results may differ from a plain program's by a relative error of at most 0.015.
Values may be sent and summed in bfloat16 or wider, within the bound.
No kernel may reach another device: no remote copies, remote signals or barrier semaphores. Data moves between devices by JAX's collectives and lax.ppermute only.
A program may use at most 128 MiB of HBM per device.

v0:
```python
import jax
import jax.numpy as jnp
from jax import lax
from jax.sharding import PartitionSpec as P


def local(inputs, out_grad, kernel, gate_weight, right_factor, left_factor):
    block = right_factor.shape[0]
    rows, width = inputs.shape
    model_width = gate_weight.shape[0]
    local_blocks = rows // block
    blocks_in = inputs.reshape(local_blocks, block, width)
    first = jnp.einsum(
        "abc,jb->ajc", blocks_in, right_factor, preferred_element_type=jnp.float32
    ).astype(jnp.bfloat16)
    scaled = (first.astype(jnp.float32) * kernel.astype(jnp.float32)).astype(jnp.bfloat16)
    piece = lax.all_to_all(scaled, "seq", split_axis=1, concat_axis=0, tiled=True)
    product = jnp.einsum("ia,ajc->jic", left_factor, piece, preferred_element_type=jnp.float32)
    mixed_cube = product.astype(jnp.bfloat16)
    mixed = mixed_cube.reshape(rows, width)
    full_weight = lax.all_gather(gate_weight, "chan", axis=1, tiled=True)
    rows_in = lax.all_to_all(inputs, "chan", split_axis=0, concat_axis=1, tiled=True)
    pre_tok = jnp.dot(rows_in, full_weight, preferred_element_type=jnp.float32)
    gate_tok = jax.nn.sigmoid(pre_tok).astype(jnp.bfloat16)
    gate = lax.all_to_all(gate_tok, "chan", split_axis=1, concat_axis=0, tiled=True)
    gate_wide = gate.astype(jnp.float32)
    cot_wide = out_grad.astype(jnp.float32)
    grad_mixed = (cot_wide * gate_wide).astype(jnp.bfloat16)
    grad_pre = (cot_wide * mixed.astype(jnp.float32) * gate_wide * (1.0 - gate_wide)).astype(
        jnp.bfloat16
    )
    pre_rows = lax.all_to_all(grad_pre, "chan", split_axis=0, concat_axis=1, tiled=True)
    gate_in_rows = jnp.einsum(
        "nk,dk->nd", pre_rows, full_weight, preferred_element_type=jnp.float32
    ).astype(jnp.bfloat16)
    weight_raw = jnp.einsum("nd,nk->dk", rows_in, pre_rows, preferred_element_type=jnp.float32)
    gate_input_grad = lax.all_to_all(gate_in_rows, "chan", split_axis=1, concat_axis=0, tiled=True)
    grad_cube = grad_mixed.reshape(local_blocks, block, width)
    grad_mid = jnp.einsum(
        "ia,jic->ajc", left_factor, grad_cube, preferred_element_type=jnp.float32
    ).astype(jnp.bfloat16)
    left_raw = jnp.einsum("jic,ajc->ia", grad_cube, piece, preferred_element_type=jnp.float32)
    grad_blocks = lax.all_to_all(grad_mid, "seq", split_axis=0, concat_axis=1, tiled=True)
    grad_wide = grad_blocks.astype(jnp.float32)
    grad_first = (grad_wide * kernel.astype(jnp.float32)).astype(jnp.bfloat16)
    kernel_grad = (grad_wide * first.astype(jnp.float32)).astype(jnp.bfloat16)
    right_raw = jnp.einsum("ajc,abc->jb", grad_first, blocks_in, preferred_element_type=jnp.float32)
    back = jnp.einsum(
        "ajc,jb->abc", grad_first, right_factor, preferred_element_type=jnp.float32
    ).reshape(rows, width)
    input_grad = (back + gate_input_grad.astype(jnp.float32)).astype(jnp.bfloat16)
    right_flat = right_raw.reshape(block * block)
    left_flat = left_raw.reshape(block * block)
    right_share, left_share, weight_share = (
        lax.psum_scatter(right_flat, ("seq", "chan"), scatter_dimension=0, tiled=True),
        lax.psum_scatter(left_flat, ("seq", "chan"), scatter_dimension=0, tiled=True),
        lax.psum_scatter(weight_raw, ("seq", "chan"), scatter_dimension=0, tiled=True),
    )
    factor_scale = 1.0 / jnp.sqrt(jnp.float32(block * model_width))
    token_scale = 1.0 / jnp.sqrt(jnp.float32(block * block))
    return (
        input_grad,
        kernel_grad,
        right_share * factor_scale,
        left_share * factor_scale,
        weight_share * token_scale,
    )


def solution(mesh):
    in_specs = (
        P("seq", "chan"),
        P("seq", "chan"),
        P("seq", None, "chan"),
        P(None, "chan"),
        P(),
        P(),
    )
    out_specs = (
        P("seq", "chan"),
        P("seq", None, "chan"),
        P(("seq", "chan")),
        P(("seq", "chan")),
        P(("seq", "chan"), None),
    )
    return jax.shard_map(local, mesh=mesh, in_specs=in_specs, out_specs=out_specs, check_vma=False)
```

profile of v0, /device:TPU:2, one launch (start us, length us, event | category | flops | bytes accessed | tf_op | source)
XLA Modules:
  0.0 548.6 jit_solution(11313670629219693192)
XLA Ops:
  7.2 6.2 %all-to-all-start = ((bf16[8,1024,128]{2,1,0:T(8,128)(2,1)}), bf16[8,1024,128]{2,1,0:T(8,128)(2,1)}, u32[]{:S(2)}, u32[]{:S(2)}) async-start(bf16[8,1024,128]{2,1,0:T(8,128)(2,1)} %bitcast.87), calls=%async_computation | async-start | bytes 4194304 | tf_op jit(solution)/shard_map/all_to_all | solution.py:22
  14.1 4.2 fusion.5
  21.0 21.7 %all-to-all-done = bf16[8,1024,128]{2,1,0:T(8,128)(2,1)} async-done(((bf16[8,1024,128]{2,1,0:T(8,128)(2,1)}), bf16[8,1024,128]{2,1,0:T(8,128)(2,1)}, u32[]{:S(2)}, u32[]{:S(2)}) %all-to-all-start) | async-done | bytes 2097184 | tf_op jit(solution)/shard_map/all_to_all | solution.py:22
  42.7 10.1 %all-to-all-start.3 = ((bf16[16,512,128]{2,0,1:T(8,128)(2,1)}), bf16[16,512,128]{2,0,1:T(8,128)(2,1)}, u32[]{:S(2)}, u32[]{:S(2)}) async-start(bf16[16,512,128]{2,0,1:T(8,128)(2,1)} %copy.67), calls=%async_computation.3 | async-start | bytes 4194304 | tf_op jit(solution)/shard_map/all_to_all | solution.py:17
  52.8 3.9 copy.60
  56.8 35.6 %all-gather.2.cloned.1.call-done = bf16[1024,1024]{1,0:T(8,128)(2,1)} async-done(((bf16[1024,128]{1,0:T(8,128)(2,1)}), bf16[1024,1024]{1,0:T(8,128)(2,1)}) %all-gather.2.cloned.1.call-update) | async-done | bytes 2097168 | tf_op jit(solution)/shard_map/all_gather | solution.py:21
  92.4 6.5 %divide_convert_fusion = bf16[1024,1024]{0,1:T(8,128)(2,1)} fusion(bf16[1024,1024]{0,1:T(8,128)(2,1)} %bitcast.97, bf16[1024,1024]{1,0:T(8,128)(2,1)} %all-gather.2.cloned.1.call-done), kind=kOutput, calls=%fused_computation.19 | convolution fusion | flops 2151677952 | bytes 6291456 | tf_op jit(solution)/shard_map/dot_general | solution.py:23
  101.9 4.4 all-to-all-start.1
  109.9 3.4 convert_bitcast_fusion.2
  113.2 5.3 copy.71
  118.5 14.5 %all-to-all-done.1 = bf16[1024,8,128]{0,2,1:T(8,128)(2,1)} async-done(((bf16[1024,8,128]{0,2,1:T(8,128)(2,1)}), bf16[1024,8,128]{0,2,1:T(8,128)(2,1)}, u32[]{:S(2)}, u32[]{:S(2)}) %all-to-all-start.1) | async-done | bytes 2097184 | tf_op jit(solution)/shard_map/all_to_all | solution.py:25
  133.1 4.1 convert_bitcast_fusion.3
  137.1 5.4 copy.61
  142.5 7.2 %fusion = (bf16[8192,128]{1,0:T(8,128)(2,1)}, bf16[8192,128]{1,0:T(8,128)(2,1)}) fusion(bf16[8192,128]{1,0:T(8,128)(2,1)} %param.7, f32[8,1024,128]{2,1,0:T(8,128)} %copy.61, f32[16,512,128]{2,1,0:T(8,128)} %copy.71), kind=kLoop, calls=%fused_computation.4 | loop fusion | flops 8388608 | bytes 14680064 | tf_op jit(solution)/shard_map/convert_element_type | solution.py:28
  149.7 4.0 copy.72
  153.7 4.7 all-to-all-start.4
  158.5 4.2 convert_bitcast_fusion.4
  162.7 4.6 copy.63
  167.3 17.9 %all-to-all-done.4 = bf16[8,1024,128]{1,2,0:T(8,128)(2,1)} async-done(((bf16[8,1024,128]{1,2,0:T(8,128)(2,1)}), bf16[8,1024,128]{1,2,0:T(8,128)(2,1)}, u32[]{:S(2)}, u32[]{:S(2)}) %all-to-all-start.4) | async-done | bytes 2097184 | tf_op jit(solution)/shard_map/all_to_all | solution.py:32
  185.2 6.1 %all-to-all-start.2 = ((bf16[512,16,128]{2,1,0:T(8,128)(2,1)}), bf16[512,16,128]{2,1,0:T(8,128)(2,1)}, u32[]{:S(2)}, u32[]{:S(2)}) async-start(bf16[512,16,128]{2,1,0:T(8,128)(2,1)} %copy.63), calls=%async_computation.2 | async-start | bytes 4194304 | tf_op jit(solution)/shard_map/all_to_all | solution.py:43
  191.3 3.5 fusion.11
  196.8 5.3 convolution_convert_fusion
  202.0 38.3 %all-to-all-done.2 = bf16[512,16,128]{2,1,0:T(8,128)(2,1)} async-done(((bf16[512,16,128]{2,1,0:T(8,128)(2,1)}), bf16[512,16,128]{2,1,0:T(8,128)(2,1)}, u32[]{:S(2)}, u32[]{:S(2)}) %all-to-all-start.2) | async-done | bytes 2097184 | tf_op jit(solution)/shard_map/all_to_all | solution.py:43
  240.3 4.8 all-to-all-start.5
  245.2 6.5 %convolution_bitcast_fusion = f32[1024,1024]{0,1:T(8,128)} fusion(bf16[1024,1024]{0,1:T(8,128)(2,1)} %bitcast.25, bf16[1024,1024]{0,1:T(8,128)(2,1)} %bitcast.98), kind=kOutput, calls=%fused_computation.20 | convolution fusion | flops 2147483648 | bytes 8388608 | tf_op jit(solution)/shard_map/nd,nk->dk/dot_general | solution.py:36
  261.3 10.4 %all-to-all-done.5 = bf16[1024,8,128]{0,2,1:T(8,128)(2,1)} async-done(((bf16[1024,8,128]{0,2,1:T(8,128)(2,1)}), bf16[1024,8,128]{0,2,1:T(8,128)(2,1)}, u32[]{:S(2)}, u32[]{:S(2)}) %all-to-all-start.5) | async-done | bytes 2097184 | tf_op jit(solution)/shard_map/all_to_all | solution.py:37
  271.7 4.3 convert_bitcast_fusion.1
  276.0 5.5 %copy.73 = f32[8,1024,128]{2,1,0:T(8,128)} copy(f32[8,1024,128]{1,2,0:T(8,128)} %convert_bitcast_fusion.1) | data formatting | bytes 8388608 | tf_op jit(solution)/shard_map/convert_element_type | solution.py:51
  281.5 3.2 convolution_bitcast_fusion.1
  284.7 5.4 copy.66
  290.1 5.3 fusion.6
  295.4 243.0 %all-reduce.6.cloned.1.call-done = (f32[262144]{0:T(1024)}, f32[262144]{0:T(1024)}, f32[1024,1024]{0,1:T(8,128)}) async-done(((f32[262144]{0:T(1024)}, f32[262144]{0:T(1024)}, f32[1024,1024]{0,1:T(8,128)}), (f32[262144]{0:T(1024)}, f32[262144]{0:T(1024)}, f32[1024,1024]{0,1:T(8,128)})) %all-reduce.6.cloned.1.call-update) | async-done | bytes 6291472
  (34 shorter events, 24.9 us)
Async XLA Ops:
  7.2 6.9 %copy-start = (bf16[512,512]{1,0:T(8,128)(2,1)S(1)}, bf16[512,512]{1,0:T(8,128)(2,1)}, u32[]{:S(2)}) copy-start(bf16[512,512]{1,0:T(8,128)(2,1)} %param.10) | copy-start | bytes 1572868
  7.2 6.9 %copy-start.1 = (bf16[8192,128]{1,0:T(8,128)(2,1)S(1)}, bf16[8192,128]{1,0:T(8,128)(2,1)}, u32[]{:S(2)}) copy-start(bf16[8192,128]{1,0:T(8,128)(2,1)} %param.6) | copy-start | bytes 6291460
  7.2 35.5 %all-to-all-start = ((bf16[8,1024,128]{2,1,0:T(8,128)(2,1)}), bf16[8,1024,128]{2,1,0:T(8,128)(2,1)}, u32[]{:S(2)}, u32[]{:S(2)}) async-start(bf16[8,1024,128]{2,1,0:T(8,128)(2,1)} %bitcast.87), calls=%async_computation | async-start | bytes 4194304 | tf_op jit(solution)/shard_map/all_to_all | solution.py:22
  13.4 79.0 %all-gather.2.cloned.1.call-start = ((), (), s32[]{:S(2)}) async-start(), calls=%async_computation.6 | async-start | bytes 2359296 | tf_op jit(solution)/shard_map/all_gather | solution.py:21
  42.7 59.2 %all-to-all-start.3 = ((bf16[16,512,128]{2,0,1:T(8,128)(2,1)}), bf16[16,512,128]{2,0,1:T(8,128)(2,1)}, u32[]{:S(2)}, u32[]{:S(2)}) async-start(bf16[16,512,128]{2,0,1:T(8,128)(2,1)} %copy.67), calls=%async_computation.3 | async-start | bytes 4194304 | tf_op jit(solution)/shard_map/all_to_all | solution.py:17
  101.9 31.1 %all-to-all-start.1 = ((bf16[1024,8,128]{0,2,1:T(8,128)(2,1)}), bf16[1024,8,128]{0,2,1:T(8,128)(2,1)}, u32[]{:S(2)}, u32[]{:S(2)}) async-start(bf16[1024,8,128]{0,2,1:T(8,128)(2,1)} %bitcast.100), calls=%async_computation.1 | async-start | bytes 4194304 | tf_op jit(solution)/shard_map/all_to_all | solution.py:25
  106.3 3.6 copy-start.7
  108.5 1.4 copy-start.4
  153.7 31.4 %all-to-all-start.4 = ((bf16[8,1024,128]{1,2,0:T(8,128)(2,1)}), bf16[8,1024,128]{1,2,0:T(8,128)(2,1)}, u32[]{:S(2)}, u32[]{:S(2)}) async-start(bf16[8,1024,128]{1,2,0:T(8,128)(2,1)} %copy.72), calls=%async_computation.4 | async-start | bytes 4194304 | tf_op jit(solution)/shard_map/all_to_all | solution.py:32
  185.2 55.2 %all-to-all-start.2 = ((bf16[512,16,128]{2,1,0:T(8,128)(2,1)}), bf16[512,16,128]{2,1,0:T(8,128)(2,1)}, u32[]{:S(2)}, u32[]{:S(2)}) async-start(bf16[512,16,128]{2,1,0:T(8,128)(2,1)} %copy.63), calls=%async_computation.2 | async-start | bytes 4194304 | tf_op jit(solution)/shard_map/all_to_all | solution.py:43
  194.8 2.0 copy-start.8
  240.3 31.3 %all-to-all-start.5 = ((bf16[1024,8,128]{0,2,1:T(8,128)(2,1)}), bf16[1024,8,128]{0,2,1:T(8,128)(2,1)}, u32[]{:S(2)}, u32[]{:S(2)}) async-start(bf16[1024,8,128]{0,2,1:T(8,128)(2,1)} %bitcast.99), calls=%async_computation.5 | async-start | bytes 4194304 | tf_op jit(solution)/shard_map/all_to_all | solution.py:37
  245.1 293.3 %all-reduce.6.cloned.1.call-start = ((), (), s32[]{:S(2)}) async-start(), calls=%async_computation.7 | async-start | bytes 12582912
  253.8 1.6 copy-start.2
  253.8 2.2 copy-start.3
  258.6 1.3 copy-start.5
  276.0 5.5 %copy-start.6 = (bf16[16,512,128]{2,1,0:T(8,128)(2,1)S(1)}, bf16[16,512,128]{2,1,0:T(8,128)(2,1)}, u32[]{:S(2)}) copy-start(bf16[16,512,128]{2,1,0:T(8,128)(2,1)} %copy-done.5) | copy-start | bytes 6291460
Sparse Core Ops, SparseCore 0:
  16.6 75.7 all-gather.1
  261.4 276.9 all-reduce.5
where the time goes:
time: 550 us; the launch traced here: 549 us
  waiting for transfers between devices  385 us (70%)
  local copies, waits for them, and re-layouts  46.7 us (8%)
  matrix products  38.1 us (7%)
  starting transfers between devices  36.4 us (7%)
  other arithmetic  28.1 us (5%)
  between operations  14.2 us (3%)
    unnamed x3, waiting for transfers between devices  244 us
    all_to_all x1, waiting for transfers between devices, local(): lax.all_to_all(grad_mid, 'seq', split_axis=0, concat_axis=1, tiled=True)  38.3 us
    all_gather x1, waiting for transfers between devices, local(): full_weight = lax.all_gather(gate_weight, 'chan', axis=1, tiled=True)  35.6 us
    all_to_all x1, waiting for transfers between devices, local(): lax.all_to_all(inputs, 'chan', split_axis=0, concat_axis=1, tiled=True)  21.7 us
    all_to_all x1, waiting for transfers between devices, local(): lax.all_to_all(grad_pre, 'chan', split_axis=0, concat_axis=1, tiled=True)  17.9 us
    all_to_all x1, waiting for transfers between devices, local(): lax.all_to_all(gate_tok, 'chan', split_axis=1, concat_axis=0, tiled=True)  14.5 us
  transfers between devices with their start and end apart: 8, of which 8 were waited for; matrix products, arithmetic and copies ran while one was open for 16% of the time, Pallas kernels for 0%

commit v1 on v0

--- a/solution.py
+++ b/solution.py
@@ -19,7 +19,19 @@
     mixed_cube = product.astype(jnp.bfloat16)
     mixed = mixed_cube.reshape(rows, width)
     full_weight = lax.all_gather(gate_weight, "chan", axis=1, tiled=True)
-    rows_in = lax.all_to_all(inputs, "chan", split_axis=0, concat_axis=1, tiled=True)
+
+    def proceed_the_rates(k_dim, x_part, dim_k):
+        return jnp.concatenate(
+            jax.lax.all_to_all(
+                jnp.stack(jnp.split(x_part, jax.lax.axis_size("chan"), axis=dim_k), axis=0),
+                axis_name="chan",
+                split_axis=0,
+                concat_axis=0,
+            ),
+            axis=k_dim,
+        )
+
+    rows_in = proceed_the_rates(1, inputs, 0)
     pre_tok = jnp.dot(rows_in, full_weight, preferred_element_type=jnp.float32)
     gate_tok = jax.nn.sigmoid(pre_tok).astype(jnp.bfloat16)
     gate = lax.all_to_all(gate_tok, "chan", split_axis=1, concat_axis=0, tiled=True)

time: 550 us -> 558 us (1.015)
    unnamed x21 -> x35, local copies, waits for them, and re-layouts: 7.27 us -> 12.7 us
  transfers between devices with their start and end apart: 8 -> 8, of which waited for: 8 -> 8; matrix products, arithmetic and copies ran while one was open for 16% -> 15% of each run, Pallas kernels for 0% -> 0%
where the time goes in v1:
time: 558 us; the launch traced here: 557 us
  waiting for transfers between devices  389 us (70%)
  local copies, waits for them, and re-layouts  50.5 us (9%)
  matrix products  38.2 us (7%)
  starting transfers between devices  36.7 us (7%)
  other arithmetic  28.1 us (5%)
  between operations  14.2 us (3%)
    unnamed x3, waiting for transfers between devices  244 us
    all_gather x1, waiting for transfers between devices, local(): full_weight = lax.all_gather(gate_weight, 'chan', axis=1, tiled=True)  39.5 us
    all_to_all x1, waiting for transfers between devices, local(): lax.all_to_all(grad_mid, 'seq', split_axis=0, concat_axis=1, tiled=True)  38.4 us
    all_to_all x1, waiting for transfers between devices, proceed_the_rates(): jax.lax.all_to_all(jnp.stack(jnp.split(x_part, jax.lax.axis_size('chan'),...  21.7 us
    all_to_all x1, waiting for transfers between devices, local(): lax.all_to_all(grad_pre, 'chan', split_axis=0, concat_axis=1, tiled=True)  17.9 us
    all_to_all x1, waiting for transfers between devices, local(): lax.all_to_all(gate_tok, 'chan', split_axis=1, concat_axis=0, tiled=True)  14.4 us
    unnamed x35, local copies, waits for them, and re-layouts  12.7 us
  transfers between devices with their start and end apart: 8, of which 8 were waited for; matrix products, arithmetic and copies ran while one was open for 15% of the time, Pallas kernels for 0%

profile of v1, /device:TPU:2, one launch (start us, length us, event | category | flops | bytes accessed | tf_op | source)
XLA Modules:
  0.0 556.6 jit_solution(3980552262787834899)
XLA Ops:
  15.9 6.2 %all-to-all-start = ((bf16[8,1024,128]{1,2,0:T(8,128)(2,1)}), bf16[8,1024,128]{1,2,0:T(8,128)(2,1)}, u32[]{:S(2)}, u32[]{:S(2)}) async-start(bf16[8,1024,128]{1,2,0:T(8,128)(2,1)} %bitcast_dynamic-update-slice_fusion), calls=%async_computation | async-start | bytes 4194304 | tf_op jit(solution)/shard_map/all_to_all | solution.py:25
  22.8 4.2 fusion.5
  29.7 21.7 %all-to-all-done = bf16[8,1024,128]{1,2,0:T(8,128)(2,1)} async-done(((bf16[8,1024,128]{1,2,0:T(8,128)(2,1)}), bf16[8,1024,128]{1,2,0:T(8,128)(2,1)}, u32[]{:S(2)}, u32[]{:S(2)}) %all-to-all-start) | async-done | bytes 2097184 | tf_op jit(solution)/shard_map/all_to_all | solution.py:25
  51.4 10.1 %all-to-all-start.3 = ((bf16[16,512,128]{2,0,1:T(8,128)(2,1)}), bf16[16,512,128]{2,0,1:T(8,128)(2,1)}, u32[]{:S(2)}, u32[]{:S(2)}) async-start(bf16[16,512,128]{2,0,1:T(8,128)(2,1)} %copy.72), calls=%async_computation.3 | async-start | bytes 4194304 | tf_op jit(solution)/shard_map/all_to_all | solution.py:17
  61.5 39.5 %all-gather.2.cloned.1.call-done = bf16[1024,1024]{1,0:T(8,128)(2,1)} async-done(((bf16[1024,128]{1,0:T(8,128)(2,1)}), bf16[1024,1024]{1,0:T(8,128)(2,1)}) %all-gather.2.cloned.1.call-update) | async-done | bytes 2097168 | tf_op jit(solution)/shard_map/all_gather | solution.py:21
  101.1 6.5 %divide_convert_fusion = bf16[1024,1024]{0,1:T(8,128)(2,1)} fusion(bf16[1024,1024]{0,1:T(8,128)(2,1)} %bitcast.9, bf16[1024,1024]{1,0:T(8,128)(2,1)} %all-gather.2.cloned.1.call-done), kind=kOutput, calls=%fused_computation.19 | convolution fusion | flops 2151677952 | bytes 6291456 | tf_op jit(solution)/shard_map/dot_general | solution.py:35
  107.6 3.0 all-to-all-done.3
  110.6 4.5 all-to-all-start.1
  118.7 3.4 convert_bitcast_fusion.2
  122.1 5.3 copy.76
  127.4 14.4 %all-to-all-done.1 = bf16[1024,8,128]{0,2,1:T(8,128)(2,1)} async-done(((bf16[1024,8,128]{0,2,1:T(8,128)(2,1)}), bf16[1024,8,128]{0,2,1:T(8,128)(2,1)}, u32[]{:S(2)}, u32[]{:S(2)}) %all-to-all-start.1) | async-done | bytes 2097184 | tf_op jit(solution)/shard_map/all_to_all | solution.py:37
  141.7 4.0 convert_bitcast_fusion.3
  145.8 5.4 copy.66
  151.2 7.2 %fusion = (bf16[8192,128]{1,0:T(8,128)(2,1)}, bf16[8192,128]{1,0:T(8,128)(2,1)}) fusion(bf16[8192,128]{1,0:T(8,128)(2,1)} %param.7, f32[8,1024,128]{2,1,0:T(8,128)} %copy.66, f32[16,512,128]{2,1,0:T(8,128)} %copy.76), kind=kLoop, calls=%fused_computation.4 | loop fusion | flops 8388608 | bytes 14680064 | tf_op jit(solution)/shard_map/convert_element_type | solution.py:40
  158.4 3.9 copy.77
  162.3 4.7 all-to-all-start.4
  167.0 4.3 convert_bitcast_fusion.4
  171.3 4.5 copy.68
  175.8 17.9 %all-to-all-done.4 = bf16[8,1024,128]{1,2,0:T(8,128)(2,1)} async-done(((bf16[8,1024,128]{1,2,0:T(8,128)(2,1)}), bf16[8,1024,128]{1,2,0:T(8,128)(2,1)}, u32[]{:S(2)}, u32[]{:S(2)}) %all-to-all-start.4) | async-done | bytes 2097184 | tf_op jit(solution)/shard_map/all_to_all | solution.py:44
  193.8 6.1 %all-to-all-start.2 = ((bf16[512,16,128]{2,1,0:T(8,128)(2,1)}), bf16[512,16,128]{2,1,0:T(8,128)(2,1)}, u32[]{:S(2)}, u32[]{:S(2)}) async-start(bf16[512,16,128]{2,1,0:T(8,128)(2,1)} %copy.68), calls=%async_computation.2 | async-start | bytes 4194304 | tf_op jit(solution)/shard_map/all_to_all | solution.py:55
  199.9 3.5 fusion.11
  205.4 5.2 convolution_convert_fusion
  210.6 38.4 %all-to-all-done.2 = bf16[512,16,128]{2,1,0:T(8,128)(2,1)} async-done(((bf16[512,16,128]{2,1,0:T(8,128)(2,1)}), bf16[512,16,128]{2,1,0:T(8,128)(2,1)}, u32[]{:S(2)}, u32[]{:S(2)}) %all-to-all-start.2) | async-done | bytes 2097184 | tf_op jit(solution)/shard_map/all_to_all | solution.py:55
  248.9 4.8 all-to-all-start.5
  254.0 6.6 %fusion.19 = f32[1024,1024]{1,0:T(8,128)} fusion(bf16[1024,1024]{0,1:T(8,128)(2,1)} %bitcast.9, bf16[1024,1024]{0,1:T(8,128)(2,1)} %bitcast.32), kind=kOutput, calls=%fused_computation.45 | convolution fusion | flops 2147483648 | bytes 8388608 | tf_op jit(solution)/shard_map/nd,nk->dk/dot_general | solution.py:48
  270.2 10.1 %all-to-all-done.5 = bf16[1024,8,128]{0,2,1:T(8,128)(2,1)} async-done(((bf16[1024,8,128]{0,2,1:T(8,128)(2,1)}), bf16[1024,8,128]{0,2,1:T(8,128)(2,1)}, u32[]{:S(2)}, u32[]{:S(2)}) %all-to-all-start.5) | async-done | bytes 2097184 | tf_op jit(solution)/shard_map/all_to_all | solution.py:49
  280.3 4.2 convert_bitcast_fusion.1
  284.5 5.5 copy.78
  290.1 3.3 convolution_bitcast_fusion
  293.3 5.4 copy.71
  298.7 5.3 fusion.6
  304.0 243.1 %all-reduce.6.cloned.1.call-done = (f32[262144]{0:T(1024)}, f32[262144]{0:T(1024)}, f32[1024,1024]{1,0:T(8,128)}) async-done(((f32[262144]{0:T(1024)}, f32[262144]{0:T(1024)}, f32[1024,1024]{1,0:T(8,128)}), (f32[262144]{0:T(1024)}, f32[262144]{0:T(1024)}, f32[1024,1024]{1,0:T(8,128)})) %all-reduce.6.cloned.1.call-update) | async-done | bytes 6291472
  (49 shorter events, 30.0 us)
Async XLA Ops:
  7.2 15.6 %copy-start = (bf16[512,512]{1,0:T(8,128)(2,1)S(1)}, bf16[512,512]{1,0:T(8,128)(2,1)}, u32[]{:S(2)}) copy-start(bf16[512,512]{1,0:T(8,128)(2,1)} %param.10) | copy-start | bytes 1572868
  15.9 6.9 %copy-start.1 = (bf16[8192,128]{1,0:T(8,128)(2,1)S(1)}, bf16[8192,128]{1,0:T(8,128)(2,1)}, u32[]{:S(2)}) copy-start(bf16[8192,128]{1,0:T(8,128)(2,1)} %param.6) | copy-start | bytes 6291460
  15.9 35.5 %all-to-all-start = ((bf16[8,1024,128]{1,2,0:T(8,128)(2,1)}), bf16[8,1024,128]{1,2,0:T(8,128)(2,1)}, u32[]{:S(2)}, u32[]{:S(2)}) async-start(bf16[8,1024,128]{1,2,0:T(8,128)(2,1)} %bitcast_dynamic-update-slice_fusion), calls=%async_computation | async-start | bytes 4194304 | tf_op jit(solution)/shard_map/all_to_all | solution.py:25
  22.0 79.0 %all-gather.2.cloned.1.call-start = ((), (), s32[]{:S(2)}) async-start(), calls=%async_computation.6 | async-start | bytes 2359296 | tf_op jit(solution)/shard_map/all_gather | solution.py:21
  51.4 59.2 %all-to-all-start.3 = ((bf16[16,512,128]{2,0,1:T(8,128)(2,1)}), bf16[16,512,128]{2,0,1:T(8,128)(2,1)}, u32[]{:S(2)}, u32[]{:S(2)}) async-start(bf16[16,512,128]{2,0,1:T(8,128)(2,1)} %copy.72), calls=%async_computation.3 | async-start | bytes 4194304 | tf_op jit(solution)/shard_map/all_to_all | solution.py:17
  110.6 31.1 %all-to-all-start.1 = ((bf16[1024,8,128]{0,2,1:T(8,128)(2,1)}), bf16[1024,8,128]{0,2,1:T(8,128)(2,1)}, u32[]{:S(2)}, u32[]{:S(2)}) async-start(bf16[1024,8,128]{0,2,1:T(8,128)(2,1)} %bitcast.109), calls=%async_computation.1 | async-start | bytes 4194304 | tf_op jit(solution)/shard_map/all_to_all | solution.py:37
  115.2 3.6 copy-start.7
  117.4 1.3 copy-start.4
  162.3 31.4 %all-to-all-start.4 = ((bf16[8,1024,128]{1,2,0:T(8,128)(2,1)}), bf16[8,1024,128]{1,2,0:T(8,128)(2,1)}, u32[]{:S(2)}, u32[]{:S(2)}) async-start(bf16[8,1024,128]{1,2,0:T(8,128)(2,1)} %copy.77), calls=%async_computation.4 | async-start | bytes 4194304 | tf_op jit(solution)/shard_map/all_to_all | solution.py:44
  193.8 55.2 %all-to-all-start.2 = ((bf16[512,16,128]{2,1,0:T(8,128)(2,1)}), bf16[512,16,128]{2,1,0:T(8,128)(2,1)}, u32[]{:S(2)}, u32[]{:S(2)}) async-start(bf16[512,16,128]{2,1,0:T(8,128)(2,1)} %copy.68), calls=%async_computation.2 | async-start | bytes 4194304 | tf_op jit(solution)/shard_map/all_to_all | solution.py:55
  203.4 2.0 copy-start.8
  248.9 31.3 %all-to-all-start.5 = ((bf16[1024,8,128]{0,2,1:T(8,128)(2,1)}), bf16[1024,8,128]{0,2,1:T(8,128)(2,1)}, u32[]{:S(2)}, u32[]{:S(2)}) async-start(bf16[1024,8,128]{0,2,1:T(8,128)(2,1)} %bitcast.108), calls=%async_computation.5 | async-start | bytes 4194304 | tf_op jit(solution)/shard_map/all_to_all | solution.py:49
  253.7 293.4 %all-reduce.6.cloned.1.call-start = ((), (), s32[]{:S(2)}) async-start(), calls=%async_computation.7 | async-start | bytes 12582912
  262.6 1.6 copy-start.2
  262.7 2.2 copy-start.3
  267.5 1.3 copy-start.5
  284.5 5.5 copy-start.6
Sparse Core Ops, SparseCore 0:
  25.3 75.7 all-gather.1
  270.3 276.7 all-reduce.5
